TPU v7x, 128 devices: a whole 4x4x4 slice. The times are simulated.
128 devices in a mesh: sites: 8 (over x, core), rows: 16 (over z, y).
Axes of the slice: x: 4, y: 4, z: 4, core: 2. Of those that a mesh axis runs over, the one named last changes fastest.
Arguments:
- bond: bfloat16 [64, 384, 384], P('sites', 'rows')
- left_env: bfloat16 [64, 384, 5, 384], P('sites', 'rows'), as said below
- right_env: bfloat16 [64, 384, 5, 384], P('sites', 'rows'), as said below
Outputs:
- evolved: float32 [64, 384, 384], P('sites', 'rows')
Inputs may be any that keep to these rules, and one draw needn't show every extreme that they name: Each environment is symmetric in its two bond indices: left_env[b, k, a, i] = left_env[b, i, a, k]. Each environment is symmetric in its two bond indices: right_env[e, j, a, l] = right_env[e, l, a, j].
All inputs are finite; a program needn't handle non-finite values.
Results may differ from a plain program's by a relative error of at most 0.0049.
Values may be sent and summed in bfloat16 or wider, within the bound.
A program may use at most 64 MiB of HBM per device.

v0:
```python
import jax
import jax.numpy as jnp
from jax import lax
from jax.sharding import PartitionSpec as P

KRYLOV = 4


small_eps = 1e-06
tau_step = 0.5
series_terms = 24


def passed_along(block, axis, distance):
    devices = range(lax.axis_size(axis))
    route = [((i - distance) % len(devices), i) for i in devices]
    return lax.ppermute(block, axis, route)


def krylov_weights(correlations, couplings):
    length = len(correlations)
    series_term = [jnp.ones_like(correlations[0])] + [
        jnp.zeros_like(correlations[0]) for _ in range(length - 1)
    ]
    running = list(series_term)
    for order_n in range(1, series_terms + 1):
        fresh = []
        for row_idx in range(length):
            value = correlations[row_idx] * series_term[row_idx]
            if row_idx > 0:
                value = value + couplings[row_idx - 1] * series_term[row_idx - 1]
            if row_idx < length - 1:
                value = value + couplings[row_idx] * series_term[row_idx + 1]
            fresh.append(value * (tau_step / order_n))
        series_term = fresh
        running = [old + new for old, new in zip(running, series_term)]
    return running


def per_device(bond, left_env, right_env):
    bond_count = bond.shape[0]
    edge_env = passed_along(right_env[:1], "sites", -1)
    shifted = jnp.concatenate([right_env[1:], edge_env], axis=0)
    right_whole = lax.all_gather(shifted, "rows", axis=1, tiled=True)
    start_matrix = jnp.transpose(bond, (1, 0, 2)).astype(jnp.float32)
    square_local = jnp.sum(start_matrix * start_matrix, axis=(0, 2))
    norm_now = jnp.sqrt(lax.psum(square_local, "rows") + small_eps)
    vectors = [start_matrix / norm_now[None, :, None]]
    correlations = []
    couplings = []
    previous = jnp.zeros_like(start_matrix)
    coupling_prev = jnp.zeros((bond_count,), jnp.float32)
    for lanczos_step in range(KRYLOV):
        current = vectors[lanczos_step]
        rounded = current.astype(jnp.bfloat16)
        crossed = jnp.einsum(
            "kbl,bjal->bkaj", rounded, right_whole, preferred_element_type=jnp.float32
        )
        sliced = left_env.astype(jnp.float32)
        image = lax.psum_scatter(
            jnp.einsum("bkai,bkaj->ibj", sliced, crossed, precision=lax.Precision.HIGHEST),
            "rows",
            scatter_dimension=0,
            tiled=True,
        )
        correlation_now = lax.psum(jnp.sum(current * image, axis=(0, 2)), "rows")
        correlations.append(correlation_now)
        if lanczos_step + 1 < KRYLOV:
            image = (
                image
                - correlation_now[None, :, None] * current
                - coupling_prev[None, :, None] * previous
            )
            residual_sq = lax.psum(jnp.sum(image * image, axis=(0, 2)), "rows")
            coupling_now = jnp.sqrt(residual_sq + small_eps)
        if lanczos_step + 1 < KRYLOV:
            couplings.append(coupling_now)
            previous = current
            coupling_prev = coupling_now
            vectors.append(image / coupling_now[None, :, None])
    weights = krylov_weights(correlations, couplings)
    combined = weights[0][None, :, None] * vectors[0]
    for index_k in range(1, KRYLOV):
        combined = combined + weights[index_k][None, :, None] * vectors[index_k]
    square_sum = weights[0] * weights[0]
    for index_k in range(1, KRYLOV):
        square_sum = square_sum + weights[index_k] * weights[index_k]
    evolved = combined * (norm_now / jnp.sqrt(square_sum))[None, :, None]
    return jnp.transpose(evolved, (1, 0, 2))


def solution(mesh):
    placed = (
        P("sites", "rows", None),
        P("sites", "rows", None, None),
        P("sites", "rows", None, None),
    )
    return jax.shard_map(
        per_device, mesh=mesh, in_specs=placed, out_specs=P("sites", "rows", None), check_vma=False
    )
```

profile of v0, /device:TPU:0, one launch (start us, length us, event | category | flops | bytes accessed | tf_op | source)
XLA Modules:
  0.0 763.1 jit_solution(7772018413300146780)
XLA Ops:
  7.5 2.3 collective-permute-start
  14.1 42.4 %psum.56 = f32[8]{0:T(128)S(1)} all-reduce(f32[8]{0:T(128)S(1)} %fusion.4), channel_id=1, replica_groups=mesh['sites'=8,'rows'=16] {'rows'}, use_global_device_ids=true, to_apply=%region_1.0 | all-reduce | flops 8 | bytes 64 | tf_op jit(solution)/shard_map/psum | solution.py:47
  57.5 44.3 %all-gather.2.cloned.1.call-done = bf16[8,384,5,384]{3,1,2,0:T(8,128)(2,1)} async-done(((bf16[8,24,5,384]{3,1,2,0:T(8,128)(2,1)}), bf16[8,384,5,384]{3,1,2,0:T(8,128)(2,1)}) %all-gather.2.cloned.1.call-update) | async-done | bytes 11796496 | tf_op jit(solution)/shard_map/all_gather | solution.py:44
  101.9 8.5 %fusion.12 = f32[8,384,5,24]{1,3,2,0:T(8,128)S(1)} fusion(bf16[8,384,5,384]{3,1,2,0:T(8,128)(2,1)} %all-gather.2.cloned.1.call-done, bf16[24,8,384,1]{2,1,0,3:T(8,128)(2,1)S(1)} %convert_bitcast_fusion.3), kind=kOutput, calls=%fused_computation.30 | convolution fusion | flops 283115520 | bytes 13418496 | tf_op jit(solution)/shard_map/kbl,bjal->bkaj/dot_general | solution.py:56
  110.4 3.8 convolution_bitcast_fusion.3
  114.2 6.1 copy.7
  120.4 79.1 %reduce-scatter.5.cloned.1.call-done = f32[24,8,384]{2,1,0:T(8,128)} async-done(((f32[384,8,384]{2,1,0:T(8,128)}), f32[24,8,384]{2,1,0:T(8,128)}) %reduce-scatter.5.cloned.1.call-update) | async-done | bytes 294928 | tf_op jit(solution)/shard_map/reduce_scatter | solution.py:60
  199.5 1.2 multiply_reduce_fusion.6
  200.7 38.1 %psum.57 = f32[8]{0:T(128)S(1)} all-reduce(f32[8]{0:T(128)S(1)} %multiply_reduce_fusion.6), channel_id=1, replica_groups=mesh['sites'=8,'rows'=16] {'rows'}, use_global_device_ids=true, to_apply=%region_4.0 | all-reduce | flops 8 | bytes 64 | tf_op jit(solution)/shard_map/psum | solution.py:66
  238.8 1.2 multiply_reduce_fusion.5
  240.1 35.5 %psum.58 = f32[8]{0:T(128)S(1)} all-reduce(f32[8]{0:T(128)S(1)} %multiply_reduce_fusion.5), channel_id=1, replica_groups=mesh['sites'=8,'rows'=16] {'rows'}, use_global_device_ids=true, to_apply=%region_6.0 | all-reduce | flops 8 | bytes 64 | tf_op jit(solution)/shard_map/psum | solution.py:74
  276.6 8.5 %fusion.10 = f32[8,384,5,24]{1,3,2,0:T(8,128)S(1)} fusion(bf16[8,384,5,384]{3,1,2,0:T(8,128)(2,1)} %all-gather.2.cloned.1.call-done, bf16[24,8,384,1]{2,1,0,3:T(8,128)(2,1)S(1)} %get-tuple-element.47), kind=kOutput, calls=%fused_computation.28 | convolution fusion | flops 283115520 | bytes 13418496 | tf_op jit(solution)/shard_map/kbl,bjal->bkaj/dot_general | solution.py:56
  285.2 3.7 convolution_bitcast_fusion.2
  288.9 6.1 copy.8
  295.1 77.1 %reduce-scatter.7.cloned.1.call-done = f32[24,8,384]{2,1,0:T(8,128)} async-done(((f32[384,8,384]{2,1,0:T(8,128)}), f32[24,8,384]{2,1,0:T(8,128)}) %reduce-scatter.7.cloned.1.call-update) | async-done | bytes 294928 | tf_op jit(solution)/shard_map/reduce_scatter | solution.py:60
  373.4 38.1 %psum.59 = f32[8]{0:T(128)S(1)} all-reduce(f32[8]{0:T(128)S(1)} %multiply_reduce_fusion.4), channel_id=1, replica_groups=mesh['sites'=8,'rows'=16] {'rows'}, use_global_device_ids=true, to_apply=%region_9.0 | all-reduce | flops 8 | bytes 64 | tf_op jit(solution)/shard_map/psum | solution.py:66
  411.5 1.2 multiply_reduce_fusion.3
  412.8 35.7 %psum.60 = f32[8]{0:T(128)S(1)} all-reduce(f32[8]{0:T(128)S(1)} %get-tuple-element.45), channel_id=1, replica_groups=mesh['sites'=8,'rows'=16] {'rows'}, use_global_device_ids=true, to_apply=%region_11.0 | all-reduce | flops 8 | bytes 64 | tf_op jit(solution)/shard_map/psum | solution.py:74
  448.6 8.5 %fusion.8 = f32[8,384,5,24]{1,3,2,0:T(8,128)S(1)} fusion(bf16[8,384,5,384]{3,1,2,0:T(8,128)(2,1)} %all-gather.2.cloned.1.call-done, bf16[24,8,384,1]{2,1,0,3:T(8,128)(2,1)S(1)} %convert_bitcast_fusion.1), kind=kOutput, calls=%fused_computation.26 | convolution fusion | flops 283115520 | bytes 13418496 | tf_op jit(solution)/shard_map/kbl,bjal->bkaj/dot_general | solution.py:56
  457.1 3.7 convolution_bitcast_fusion.1
  460.8 6.1 copy.9
  467.0 77.1 %reduce-scatter.9.cloned.1.call-done = f32[24,8,384]{2,1,0:T(8,128)} async-done(((f32[384,8,384]{2,1,0:T(8,128)}), f32[24,8,384]{2,1,0:T(8,128)}) %reduce-scatter.9.cloned.1.call-update) | async-done | bytes 294928 | tf_op jit(solution)/shard_map/reduce_scatter | solution.py:60
  544.2 1.2 multiply_reduce_fusion.2
  545.4 38.1 %psum.61 = f32[8]{0:T(128)S(1)} all-reduce(f32[8]{0:T(128)S(1)} %multiply_reduce_fusion.2), channel_id=1, replica_groups=mesh['sites'=8,'rows'=16] {'rows'}, use_global_device_ids=true, to_apply=%region_14.0 | all-reduce | flops 8 | bytes 64 | tf_op jit(solution)/shard_map/psum | solution.py:66
  583.5 1.2 multiply_reduce_fusion.1
  584.7 35.5 %psum.62 = f32[8]{0:T(128)S(1)} all-reduce(f32[8]{0:T(128)S(1)} %get-tuple-element.43), channel_id=1, replica_groups=mesh['sites'=8,'rows'=16] {'rows'}, use_global_device_ids=true, to_apply=%region_16.0 | all-reduce | flops 8 | bytes 64 | tf_op jit(solution)/shard_map/psum | solution.py:74
  620.3 8.5 %fusion.6 = f32[8,384,5,24]{1,3,2,0:T(8,128)S(1)} fusion(bf16[8,384,5,384]{3,1,2,0:T(8,128)(2,1)} %all-gather.2.cloned.1.call-done, bf16[24,8,384,1]{2,1,0,3:T(8,128)(2,1)S(1)} %convert_bitcast_fusion), kind=kOutput, calls=%fused_computation.24 | convolution fusion | flops 283115520 | bytes 13418496 | tf_op jit(solution)/shard_map/kbl,bjal->bkaj/dot_general | solution.py:56
  628.9 3.8 convolution_bitcast_fusion
  632.7 6.1 copy.10
  638.8 77.2 %reduce-scatter.11.cloned.1.call-done = f32[24,8,384]{2,1,0:T(8,128)} async-done(((f32[384,8,384]{2,1,0:T(8,128)}), f32[24,8,384]{2,1,0:T(8,128)}) %reduce-scatter.11.cloned.1.call-update) | async-done | bytes 294928 | tf_op jit(solution)/shard_map/reduce_scatter | solution.py:60
  716.0 1.2 multiply_reduce_fusion
  717.2 38.1 %psum.63 = f32[8]{0:T(128)S(1)} all-reduce(f32[8]{0:T(128)S(1)} %multiply_reduce_fusion), channel_id=1, replica_groups=mesh['sites'=8,'rows'=16] {'rows'}, use_global_device_ids=true, to_apply=%region_19.0 | all-reduce | flops 8 | bytes 64 | tf_op jit(solution)/shard_map/psum | solution.py:66
  (32 shorter events, 10.1 us)
Async XLA Ops:
  6.5 103.9 %copy-start = (bf16[8,24,5,384]{3,1,2,0:T(8,128)(2,1)S(1)}, bf16[8,24,5,384]{3,1,2,0:T(8,128)(2,1)}, u32[]{:S(2)}) copy-start(bf16[8,24,5,384]{3,1,2,0:T(8,128)(2,1)} %param.4) | copy-start | bytes 2211844
  6.5 95.3 %all-gather.2.cloned.1.call-start = ((), (), s32[]{:S(2)}) async-start(), calls=%async_computation.4 | async-start | bytes 12533760 | tf_op jit(solution)/shard_map/all_gather | solution.py:44
  7.5 4.5 collective-permute-start
  13.0 186.5 %reduce-scatter.5.cloned.1.call-start = ((), (), s32[]{:S(2)}) async-start(), calls=%async_computation.5 | async-start | bytes 5013504 | tf_op jit(solution)/shard_map/reduce_scatter | solution.py:60
  120.3 79.2 %copy-start.1 = (bf16[8,24,384]{2,1,0:T(8,128)(2,1)S(1)}, bf16[8,24,384]{2,1,0:T(8,128)(2,1)}, u32[]{:S(2)}) copy-start(bf16[8,24,384]{2,1,0:T(8,128)(2,1)} %param.3) | copy-start | bytes 442372
  120.3 251.9 %reduce-scatter.7.cloned.1.call-start = ((), (), s32[]{:S(2)}) async-start(), calls=%async_computation.6 | async-start | bytes 5013504 | tf_op jit(solution)/shard_map/reduce_scatter | solution.py:60
  295.1 249.1 %reduce-scatter.9.cloned.1.call-start = ((), (), s32[]{:S(2)}) async-start(), calls=%async_computation.7 | async-start | bytes 5013504 | tf_op jit(solution)/shard_map/reduce_scatter | solution.py:60
  467.0 249.0 %reduce-scatter.11.cloned.1.call-start = ((), (), s32[]{:S(2)}) async-start(), calls=%async_computation.8 | async-start | bytes 5013504 | tf_op jit(solution)/shard_map/reduce_scatter | solution.py:60
Sparse Core Ops, SparseCore 0:
  13.1 88.7 all-gather.1
  120.4 78.9 reduce-scatter.4
  295.2 77.0 reduce-scatter.6
  467.1 77.0 reduce-scatter.8
  638.9 77.0 reduce-scatter.10
where the time goes:
time: 764 us; the launch traced here: 763 us
  waiting for transfers between devices  356 us (47%)
  blocking collectives  301 us (39%)
  matrix products  49.2 us (6%)
  local copies, waits for them, and re-layouts  27.4 us (4%)
  other arithmetic  13.3 us (2%)
  between operations  13.2 us (2%)
    reduce_scatter x4, waiting for transfers between devices, per_device(): lax.psum_scatter(jnp.einsum('bkai,bkaj->ibj', sliced, crossed, precision=...  311 us
    psum x4, blocking collectives, per_device(): correlation_now = lax.psum(jnp.sum(current * image, axis=(0, 2)), 'rows')  152 us
    psum x3, blocking collectives, per_device(): residual_sq = lax.psum(jnp.sum(image * image, axis=(0, 2)), 'rows')  107 us
    all_gather x1, waiting for transfers between devices, per_device(): right_whole = lax.all_gather(shifted, 'rows', axis=1, tiled=True)  44.3 us
    psum x1, blocking collectives, per_device(): norm_now = jnp.sqrt(lax.psum(square_local, 'rows') + small_eps)  42.4 us
    dot_general x4, matrix products, per_device(): jnp.einsum('kbl,bjal->bkaj', rounded, right_whole, preferred_element_type...  34.1 us
    transpose x4, local copies, waits for them, and re-layouts, per_device(): jnp.einsum('bkai,bkaj->ibj', sliced, crossed, precision=lax.Precision.HIG...  24.5 us
  transfers between devices with their start and end apart: 6, of which 6 were waited for; matrix products, arithmetic and copies ran while one was open for 0% of the time, Pallas kernels for 0%

commit v1 on v0

v1 whole, which is shorter than its diff:
```python
import jax
import jax.numpy as jnp
from jax import lax
from jax.experimental import pallas as pl
from jax.experimental.pallas import tpu as pltpu
from jax.sharding import PartitionSpec as P

KRYLOV = 4
CHI = 384
WM = 5
eps = 1e-06
tau_step = 0.5
series_terms = 24


def krylov_weights(diag, off):
    length = len(diag)
    term = [jnp.ones_like(diag[0])] + [jnp.zeros_like(diag[0])] * (length - 1)
    running = list(term)
    for n in range(1, series_terms + 1):
        fresh = []
        for i in range(length):
            value = diag[i] * term[i]
            if i > 0:
                value = value + off[i - 1] * term[i - 1]
            if i < length - 1:
                value = value + off[i] * term[i + 1]
            fresh.append(value * (tau_step / n))
        term = fresh
        running = [old + new for old, new in zip(running, term)]
    return running


def total(x):
    return jnp.sum(jnp.sum(x, axis=0, keepdims=True), axis=1, keepdims=True)


def image_of(vec, left, right):
    rounded = vec.astype(jnp.bfloat16)
    image = None
    for a in range(WM):
        cols = slice(a * CHI, (a + 1) * CHI)
        crossed = jnp.dot(rounded, right[:, cols], preferred_element_type=jnp.float32)
        high = crossed.astype(jnp.bfloat16)
        low = (crossed - high.astype(jnp.float32)).astype(jnp.bfloat16)
        part = jnp.dot(left[:, cols], high, preferred_element_type=jnp.float32)
        part = part + jnp.dot(left[:, cols], low, preferred_element_type=jnp.float32)
        image = part if image is None else image + part
    return image


def lanczos(bond, left, right, vecs, out):
    start = bond[...].astype(jnp.float32)
    norm = jnp.sqrt(total(start * start) + eps)
    vecs[0] = start / norm
    diag, off = [], []
    for k in range(KRYLOV):
        image = image_of(vecs[k], left, right)
        alpha = total(vecs[k] * image)
        diag.append(alpha)
        if k + 1 < KRYLOV:
            w = image - alpha * vecs[k]
            if k > 0:
                w = w - off[k - 1] * vecs[k - 1]
            beta = jnp.sqrt(total(w * w) + eps)
            off.append(beta)
            vecs[k + 1] = w / beta
    weights = krylov_weights(diag, off)
    square = weights[0] * weights[0]
    for k in range(1, KRYLOV):
        square = square + weights[k] * weights[k]
    scale = norm / jnp.sqrt(square)
    combined = weights[0] * vecs[0]
    for k in range(1, KRYLOV):
        combined = combined + weights[k] * vecs[k]
    out[...] = combined * scale


def kernel(bond, left, right, out, vecs):
    lanczos(bond, left, right, vecs, out)


def swap(block):
    twice = jnp.repeat(block, 2, axis=0)
    got = lax.all_to_all(twice, "rows", 0, 0, tiled=True)
    return got.reshape(CHI, got.shape[-1])


def per_device(bond, left_env, right_env):
    n = bond.shape[0]
    size = lax.axis_size("sites")
    edge = lax.ppermute(right_env[:1], "sites", [((i + 1) % size, i) for i in range(size)])
    shifted = jnp.concatenate([right_env[1:], edge], axis=0)
    left = swap(left_env.reshape(n, -1, WM * CHI))
    right = swap(shifted.reshape(n, -1, WM * CHI))
    mine = swap(bond)
    out = pl.pallas_call(
        kernel,
        out_shape=jax.ShapeDtypeStruct((CHI, CHI), jnp.float32),
        scratch_shapes=[pltpu.VMEM((KRYLOV, CHI, CHI), jnp.float32)],
        compiler_params=pltpu.CompilerParams(vmem_limit_bytes=48 * 1024 * 1024),
    )(mine, left, right)
    ranks = lax.axis_size("rows")
    back = lax.all_to_all(out.reshape(ranks, -1, CHI), "rows", 0, 0, tiled=True)
    return back[::2]


def solution(mesh):
    placed = (
        P("sites", "rows", None),
        P("sites", "rows", None, None),
        P("sites", "rows", None, None),
    )
    return jax.shard_map(
        per_device, mesh=mesh, in_specs=placed, out_specs=P("sites", "rows", None), check_vma=False
    )
```

time: 764 us -> 101 us (0.13)
  waiting for transfers between devices: 356 us -> 29.3 us
  blocking collectives: 301 us -> 38.5 us
  matrix products: 49.2 us -> 0 us
  local copies, waits for them, and re-layouts: 27.4 us -> 3.97 us
  Pallas kernels: 0 us -> 15.2 us
  other arithmetic: 13.3 us -> 0.09 us
  between operations: 13.2 us -> 0.08 us
  starting transfers between devices: 2.49 us -> 13.1 us
    reduce_scatter x4 -> x0, waiting for transfers between devices: 311 us -> none  [per_device(): lax.psum_scatter(jnp.einsum('bkai,bkaj->ibj', sliced, crossed, precision=...]
    psum x8 -> x0, blocking collectives: 301 us -> none  [the longest x4 152 us: per_device(): correlation_now = lax.psum(jnp.sum(current * image, axis=(0, 2)), 'rows')]
    dot_general x8 -> x0, matrix products: 49.2 us -> none  [the longest x4 34.1 us: per_device(): jnp.einsum('kbl,bjal->bkaj', rounded, right_whole, preferred_element_type...]
    all_gather x1 -> x0, waiting for transfers between devices: 44.3 us -> none  [per_device(): right_whole = lax.all_gather(shifted, 'rows', axis=1, tiled=True)]
    all_to_all x0 -> x2, blocking collectives: none -> 38.5 us  [the longest x1 24.1 us: swap(): got = lax.all_to_all(twice, 'rows', 0, 0, tiled=True)]
    all_to_all x0 -> x2, waiting for transfers between devices: none -> 27.1 us  [swap(): got = lax.all_to_all(twice, 'rows', 0, 0, tiled=True)]
    transpose x5 -> x0, local copies, waits for them, and re-layouts: 25.3 us -> none  [the longest x4 24.5 us: per_device(): jnp.einsum('bkai,bkaj->ibj', sliced, crossed, precision=lax.Precision.HIG...]
    pallas_call x0 -> x1, Pallas kernels: none -> 15.2 us  [per_device(): pl.pallas_call(kernel, out_shape=jax.ShapeDtypeStruct((CHI, CHI), jnp.flo...]
  transfers between devices with their start and end apart: 6 -> 3, of which waited for: 6 -> 3; matrix products, arithmetic and copies ran while one was open for 0% -> 0% of each run, Pallas kernels for 0% -> 0%
where the time goes in v1:
time: 101 us; the launch traced here: 100 us
  blocking collectives  38.5 us (38%)
  waiting for transfers between devices  29.3 us (29%)
  Pallas kernels  15.2 us (15%)
  starting transfers between devices  13.1 us (13%)
  local copies, waits for them, and re-layouts  3.97 us (4%)
    all_to_all x2, waiting for transfers between devices, swap(): got = lax.all_to_all(twice, 'rows', 0, 0, tiled=True)  27.1 us
    all_to_all x1, blocking collectives, swap(): got = lax.all_to_all(twice, 'rows', 0, 0, tiled=True)  24.1 us
    pallas_call x1, Pallas kernels, per_device(): pl.pallas_call(kernel, out_shape=jax.ShapeDtypeStruct((CHI, CHI), jnp.flo...  15.2 us
    all_to_all x1, blocking collectives, per_device(): back = lax.all_to_all(out.reshape(ranks, -1, CHI), 'rows', 0, 0, tiled=True)  14.4 us
    all_to_all x2, starting transfers between devices, swap(): got = lax.all_to_all(twice, 'rows', 0, 0, tiled=True)  12 us
    broadcast_in_dim x3, local copies, waits for them, and re-layouts, swap(): twice = jnp.repeat(block, 2, axis=0)  3.06 us
    ppermute x1, waiting for transfers between devices, per_device(): lax.ppermute(right_env[:1], 'sites', [((i + 1) % size, i) for i in range(...  2.16 us
  transfers between devices with their start and end apart: 3, of which 3 were waited for; matrix products, arithmetic and copies ran while one was open for 0% of the time, Pallas kernels for 0%

profile of v1, /device:TPU:0, one launch (start us, length us, event | category | flops | bytes accessed | tf_op | source)
XLA Modules:
  0.0 100.2 jit_solution(7698685651045830658)
XLA Ops:
  0.0 0.0 copy-start.1
  0.0 1.7 %broadcast_in_dim.9 = bf16[8,2,24,384]{3,2,1,0:T(8,128)(2,1)} broadcast(bf16[8,24,384]{2,1,0:T(8,128)(2,1)} %param.3), dimensions={0,2,3} | broadcast | bytes 442368 | tf_op jit(solution)/shard_map/broadcast_in_dim | solution.py:84
  1.7 8.2 %all-to-all-start = ((bf16[16,24,384]{2,1,0:T(8,128)(2,1)}), bf16[16,24,384]{2,1,0:T(8,128)(2,1)S(1)}, u32[]{:S(2)}, u32[]{:S(2)}) async-start(bf16[16,24,384]{2,1,0:T(8,128)(2,1)} %bitcast), calls=%async_computation | async-start | bytes 589824 | tf_op jit(solution)/shard_map/all_to_all | solution.py:85
  9.9 0.0 copy-done.1
  9.9 0.1 copy.6
  10.0 8.9 %all-to-all-done = bf16[16,24,384]{2,1,0:T(8,128)(2,1)S(1)} async-done(((bf16[16,24,384]{2,1,0:T(8,128)(2,1)}), bf16[16,24,384]{2,1,0:T(8,128)(2,1)S(1)}, u32[]{:S(2)}, u32[]{:S(2)}) %all-to-all-start) | async-done | bytes 294944 | tf_op jit(solution)/shard_map/all_to_all | solution.py:85
  18.9 1.2 %broadcast_in_dim.10 = bf16[8,2,24,1920]{3,2,1,0:T(8,128)(2,1)} broadcast(bf16[8,24,1920]{2,1,0:T(8,128)(2,1)S(1)} %bitcast.18), dimensions={0,2,3} | broadcast | bytes 2211840 | tf_op jit(solution)/shard_map/broadcast_in_dim | solution.py:84
  20.2 0.0 copy-start
  20.2 0.0 slice-start
  20.2 3.8 %all-to-all-start.1 = ((bf16[16,24,1920]{2,1,0:T(8,128)(2,1)}), bf16[16,24,1920]{2,1,0:T(8,128)(2,1)S(1)}, u32[]{:S(2)}, u32[]{:S(2)}) async-start(bf16[16,24,1920]{2,1,0:T(8,128)(2,1)} %bitcast.2), calls=%async_computation.1 | async-start | bytes 2949120 | tf_op jit(solution)/shard_map/all_to_all | solution.py:85
  24.0 0.0 copy-done
  24.0 1.1 %collective-permute-start = (bf16[1,24,5,384]{3,1,2,0:T(8,128)(2,1)S(1)}, bf16[1,24,5,384]{3,1,2,0:T(8,128)(2,1)S(1)}, u32[]{:S(2)}, u32[]{:S(2)}) collective-permute-start(bf16[1,24,5,384]{3,1,2,0:T(8,128)(2,1)S(1)} %slice.10), channel_id=1, source_target_pairs={{16,0},{32,16},{48,32},{64,48},{80,64},{96,80},{112,96},{0,112},{1... | collective-permute-start | bytes 276488 | tf_op jit(solution)/shard_map/ppermute | solution.py:92
  25.1 2.2 %collective-permute-done = bf16[1,24,5,384]{3,1,2,0:T(8,128)(2,1)S(1)} collective-permute-done((bf16[1,24,5,384]{3,1,2,0:T(8,128)(2,1)S(1)}, bf16[1,24,5,384]{3,1,2,0:T(8,128)(2,1)S(1)}, u32[]{:S(2)}, u32[]{:S(2)}) %collective-permute-start) | collective-permute-done | bytes 92192 | tf_op jit(solution)/shard_map/ppermute | solution.py:92
  27.3 0.0 slice-done
  27.3 0.1 maximum_bitcast_fusion
  27.4 0.1 copy.7
  27.4 18.2 %all-to-all-done.1 = bf16[16,24,1920]{2,1,0:T(8,128)(2,1)S(1)} async-done(((bf16[16,24,1920]{2,1,0:T(8,128)(2,1)}), bf16[16,24,1920]{2,1,0:T(8,128)(2,1)S(1)}, u32[]{:S(2)}, u32[]{:S(2)}) %all-to-all-start.1) | async-done | bytes 1474592 | tf_op jit(solution)/shard_map/all_to_all | solution.py:85
  45.6 0.1 broadcast_in_dim.11
  45.7 24.1 %all_to_all.20 = bf16[16,24,1920]{2,1,0:T(8,128)(2,1)S(1)} all-to-all(bf16[16,24,1920]{2,1,0:T(8,128)(2,1)S(1)} %bitcast.16), channel_id=1, replica_groups=mesh['sites'=8,'rows'=16] {'rows'}, dimensions={0} | all-to-all | bytes 2949120 | tf_op jit(solution)/shard_map/all_to_all | solution.py:85
  69.9 15.2 %shard_map.37 = f32[384,384]{1,0:T(8,128)S(1)} custom-call(bf16[384,384]{1,0:T(8,128)(2,1)S(1)} %bitcast.15, bf16[384,1920]{1,0:T(8,128)(2,1)S(1)} %bitcast.12, bf16[384,1920]{1,0:T(8,128)(2,1)S(1)} %bitcast.13), custom_call_target="tpu_custom_call" | custom-call | tf_op jit(solution)/shard_map/pallas_call | solution.py:97
  85.1 14.4 %all_to_all.21 = f32[16,24,384]{2,1,0:T(8,128)S(1)} all-to-all(f32[16,24,384]{2,1,0:T(8,128)S(1)} %bitcast.14), channel_id=1, replica_groups=mesh['sites'=8,'rows'=16] {'rows'}, dimensions={0} | all-to-all | bytes 1179648 | tf_op jit(solution)/shard_map/all_to_all | solution.py:104
  99.4 0.7 slice.11
  (1 shorter events, 0.0 us)
Async XLA Ops:
  0.0 9.9 %copy-start.1 = (bf16[8,24,5,384]{3,1,2,0:T(8,128)(2,1)S(1)}, bf16[8,24,5,384]{3,1,2,0:T(8,128)(2,1)}, u32[]{:S(2)}) copy-start(bf16[8,24,5,384]{3,1,2,0:T(8,128)(2,1)} %param.4) | copy-start | bytes 2211844
  1.7 17.2 %all-to-all-start = ((bf16[16,24,384]{2,1,0:T(8,128)(2,1)}), bf16[16,24,384]{2,1,0:T(8,128)(2,1)S(1)}, u32[]{:S(2)}, u32[]{:S(2)}) async-start(bf16[16,24,384]{2,1,0:T(8,128)(2,1)} %bitcast), calls=%async_computation | async-start | bytes 589824 | tf_op jit(solution)/shard_map/all_to_all | solution.py:85
  20.2 3.9 %copy-start = (bf16[8,24,5,384]{3,1,2,0:T(8,128)(2,1)S(1)}, bf16[8,24,5,384]{3,1,2,0:T(8,128)(2,1)}, u32[]{:S(2)}) copy-start(bf16[8,24,5,384]{3,1,2,0:T(8,128)(2,1)} %param.5) | copy-start | bytes 2211844
  20.2 7.1 %slice-start = ((bf16[8,24,5,384]{3,1,2,0:T(8,128)(2,1)}), bf16[7,24,5,384]{3,1,2,0:T(8,128)(2,1)S(1)}, s32[]{:S(2)}) async-start(bf16[8,24,5,384]{3,1,2,0:T(8,128)(2,1)} %param.5), calls=%async_computation.4 | async-start | bytes 1290240 | tf_op jit(solution)/shard_map/slice | solution.py:93
  20.2 25.5 %all-to-all-start.1 = ((bf16[16,24,1920]{2,1,0:T(8,128)(2,1)}), bf16[16,24,1920]{2,1,0:T(8,128)(2,1)S(1)}, u32[]{:S(2)}, u32[]{:S(2)}) async-start(bf16[16,24,1920]{2,1,0:T(8,128)(2,1)} %bitcast.2), calls=%async_computation.1 | async-start | bytes 2949120 | tf_op jit(solution)/shard_map/all_to_all | solution.py:85
  24.0 3.2 %collective-permute-start = (bf16[1,24,5,384]{3,1,2,0:T(8,128)(2,1)S(1)}, bf16[1,24,5,384]{3,1,2,0:T(8,128)(2,1)S(1)}, u32[]{:S(2)}, u32[]{:S(2)}) collective-permute-start(bf16[1,24,5,384]{3,1,2,0:T(8,128)(2,1)S(1)} %slice.10), channel_id=1, source_target_pairs={{16,0},{32,16},{48,32},{64,48},{80,64},{96,80},{112,96},{0,112},{1... | collective-permute-start | bytes 276488 | tf_op jit(solution)/shard_map/ppermute | solution.py:92
